TPU v7x, 32 devices: a whole 2x2x4 slice. The times are simulated.
32 devices in a mesh: doc: 4 (over y, x), cen: 8 (over z, core).
Axes of the slice: x: 2, y: 2, z: 4, core: 2. Of those that a mesh axis runs over, the one named last changes fastest.
Arguments:
- passages: bfloat16 [1536, 1024], P(('doc', 'cen')), may hold values from -64 to 64
- centroids: bfloat16 [8192, 1024], P('cen'), may hold values from -64 to 64
Outputs:
- assign: bfloat16 [1536, 8192], P('doc', 'cen')
- masses: float32 [8192], P('cen')
- new_centroids: float32 [8192, 1024], P('cen', 'doc')
All inputs are finite; a program needn't handle non-finite values.
Results may differ from a plain program's by a relative error of at most 0.008.
Values may be sent and summed in bfloat16 or wider, within the bound.
A program may use at most 64 MiB of HBM per device.

v0:
```python
import math
import jax
import jax.numpy as jnp
from jax import lax
from jax.sharding import PartitionSpec as P

ITERS = 3


def row_log_total(shifted):
    local_max = jnp.max(shifted, axis=1)
    peak = lax.pmax(local_max, "cen")
    total = lax.psum(jnp.sum(jnp.exp(shifted - peak[:, None]), axis=1), "cen")
    return peak + jnp.log(total)


def col_log_total(shifted):
    local_max = jnp.max(shifted, axis=0)
    peak = lax.pmax(local_max, "doc")
    total = lax.psum(jnp.sum(jnp.exp(shifted - peak[None, :]), axis=0), "doc")
    return peak + jnp.log(total)


def shards(passages, centroids):
    cen_count = lax.axis_size("cen")
    doc_count = lax.axis_size("doc")
    width = passages.shape[1]
    scale = 1.0 / math.sqrt(width)
    group_rows = lax.all_gather(passages, "cen", axis=0, tiled=True)
    scores = (
        lax.dot_general(
            group_rows, centroids, (((1,), (1,)), ((), ())), preferred_element_type=jnp.float32
        )
        * scale
    )
    local_cols = centroids.shape[0]
    total_cols = local_cols * cen_count
    total_rows = scores.shape[0] * doc_count
    log_column = math.log(total_rows / total_cols)
    col_potential = jnp.zeros((local_cols,), jnp.float32)
    for iteration in range(ITERS):
        row_potential = -row_log_total(scores + col_potential[None, :])
        col_potential = log_column - col_log_total(scores + row_potential[:, None])
    row_potential = -row_log_total(scores + col_potential[None, :])
    weights = jnp.exp(scores + row_potential[:, None] + col_potential[None, :])
    assign = (weights * total_cols).astype(jnp.bfloat16)
    raw_mass = lax.psum(jnp.sum(weights, axis=0), "doc")
    partial_value = lax.dot_general(
        assign, group_rows, (((0,), (0,)), ((), ())), preferred_element_type=jnp.float32
    )
    sums = lax.psum_scatter(
        partial_value.astype(jnp.bfloat16), "doc", scatter_dimension=1, tiled=True
    ).astype(jnp.float32)
    new_centroids = sums / total_cols / raw_mass[:, None]
    masses = raw_mass * total_cols / total_rows
    return (assign, masses, new_centroids)


def solution(mesh):
    in_specs = (P(("doc", "cen"), None), P("cen", None))
    out_specs = (P("doc", "cen"), P("cen"), P("cen", "doc"))
    return jax.shard_map(shards, mesh=mesh, in_specs=in_specs, out_specs=out_specs, check_vma=False)
```

profile of v0, /device:TPU:0, one launch (start us, length us, event | category | flops | bytes accessed | tf_op | source)
XLA Modules:
  0.0 261.0 jit_solution(13473562070455772774)
XLA Ops:
  7.2 0.0 copy-start
  7.2 0.0 reduce-scatter.2.cloned.1.call-start
  7.2 17.6 %all_gather.3 = bf16[384,1024]{1,0:T(8,128)(2,1)S(1)} all-gather(bf16[48,1024]{1,0:T(8,128)(2,1)} %param.2), channel_id=1, replica_groups=mesh['doc'=4,'cen'=8] {'cen'}, dimensions={0}, use_global_device_ids=true | all-gather | bytes 884736 | tf_op jit(solution)/shard_map/all_gather | solution.py:29
  24.8 0.0 copy-done
  24.8 2.2 fusion.1
  27.0 17.0 %pmax.49 = f32[384]{0:T(512)S(1)} all-reduce(f32[384]{0:T(512)S(1)} %get-tuple-element.5), channel_id=1, replica_groups=mesh['doc'=4,'cen'=8] {'cen'}, use_global_device_ids=true, to_apply=%region_1.0 | all-reduce | flops 384 | bytes 3072 | tf_op jit(solution)/shard_map/pmax | solution.py:12
  44.0 1.8 exponential_reduce_fusion.6
  45.8 13.6 %psum.56 = f32[384]{0:T(512)S(1)} all-reduce(f32[384]{0:T(512)S(1)} %exponential_reduce_fusion.6), channel_id=1, replica_groups=mesh['doc'=4,'cen'=8] {'cen'}, use_global_device_ids=true, to_apply=%region_3.0 | all-reduce | flops 384 | bytes 3072 | tf_op jit(solution)/shard_map/psum | solution.py:13
  59.4 1.6 add_reduce_fusion.5
  61.0 9.9 %pmax.50 = f32[1024]{0:T(1024)S(1)} all-reduce(f32[1024]{0:T(1024)S(1)} %add_reduce_fusion.5), channel_id=1, replica_groups=mesh['doc'=4,'cen'=8] {'doc'}, use_global_device_ids=true, to_apply=%region_5.0 | all-reduce | flops 1024 | bytes 8192 | tf_op jit(solution)/shard_map/pmax | solution.py:19
  70.9 1.7 exponential_reduce_fusion.5
  72.7 8.0 %psum.57 = f32[1024]{0:T(1024)S(1)} all-reduce(f32[1024]{0:T(1024)S(1)} %exponential_reduce_fusion.5), channel_id=1, replica_groups=mesh['doc'=4,'cen'=8] {'doc'}, use_global_device_ids=true, to_apply=%region_7.0 | all-reduce | flops 1024 | bytes 8192 | tf_op jit(solution)/shard_map/psum | solution.py:20
  80.7 1.6 add_reduce_fusion.4
  82.3 13.6 %pmax.51 = f32[384]{0:T(512)S(1)} all-reduce(f32[384]{0:T(512)S(1)} %add_reduce_fusion.4), channel_id=1, replica_groups=mesh['doc'=4,'cen'=8] {'cen'}, use_global_device_ids=true, to_apply=%region_9.0 | all-reduce | flops 384 | bytes 3072 | tf_op jit(solution)/shard_map/pmax | solution.py:12
  95.8 1.8 exponential_reduce_fusion.4
  97.7 13.6 %psum.58 = f32[384]{0:T(512)S(1)} all-reduce(f32[384]{0:T(512)S(1)} %exponential_reduce_fusion.4), channel_id=1, replica_groups=mesh['doc'=4,'cen'=8] {'cen'}, use_global_device_ids=true, to_apply=%region_11.0 | all-reduce | flops 384 | bytes 3072 | tf_op jit(solution)/shard_map/psum | solution.py:13
  111.3 1.6 add_reduce_fusion.3
  112.8 9.0 %pmax.52 = f32[1024]{0:T(1024)S(1)} all-reduce(f32[1024]{0:T(1024)S(1)} %add_reduce_fusion.3), channel_id=1, replica_groups=mesh['doc'=4,'cen'=8] {'doc'}, use_global_device_ids=true, to_apply=%region_13.0 | all-reduce | flops 1024 | bytes 8192 | tf_op jit(solution)/shard_map/pmax | solution.py:19
  121.8 1.7 exponential_reduce_fusion.3
  123.6 8.0 %psum.59 = f32[1024]{0:T(1024)S(1)} all-reduce(f32[1024]{0:T(1024)S(1)} %exponential_reduce_fusion.3), channel_id=1, replica_groups=mesh['doc'=4,'cen'=8] {'doc'}, use_global_device_ids=true, to_apply=%region_15.0 | all-reduce | flops 1024 | bytes 8192 | tf_op jit(solution)/shard_map/psum | solution.py:20
  131.6 1.6 add_reduce_fusion.2
  133.2 13.6 %pmax.53 = f32[384]{0:T(512)S(1)} all-reduce(f32[384]{0:T(512)S(1)} %add_reduce_fusion.2), channel_id=1, replica_groups=mesh['doc'=4,'cen'=8] {'cen'}, use_global_device_ids=true, to_apply=%region_17.0 | all-reduce | flops 384 | bytes 3072 | tf_op jit(solution)/shard_map/pmax | solution.py:12
  146.8 1.8 exponential_reduce_fusion.2
  148.6 13.6 %psum.60 = f32[384]{0:T(512)S(1)} all-reduce(f32[384]{0:T(512)S(1)} %exponential_reduce_fusion.2), channel_id=1, replica_groups=mesh['doc'=4,'cen'=8] {'cen'}, use_global_device_ids=true, to_apply=%region_19.0 | all-reduce | flops 384 | bytes 3072 | tf_op jit(solution)/shard_map/psum | solution.py:13
  162.2 1.6 add_reduce_fusion.1
  163.8 9.7 %pmax.54 = f32[1024]{0:T(1024)S(1)} all-reduce(f32[1024]{0:T(1024)S(1)} %add_reduce_fusion.1), channel_id=1, replica_groups=mesh['doc'=4,'cen'=8] {'doc'}, use_global_device_ids=true, to_apply=%region_21.0 | all-reduce | flops 1024 | bytes 8192 | tf_op jit(solution)/shard_map/pmax | solution.py:19
  173.5 1.7 exponential_reduce_fusion.1
  175.3 8.0 %psum.61 = f32[1024]{0:T(1024)S(1)} all-reduce(f32[1024]{0:T(1024)S(1)} %exponential_reduce_fusion.1), channel_id=1, replica_groups=mesh['doc'=4,'cen'=8] {'doc'}, use_global_device_ids=true, to_apply=%region_23.0 | all-reduce | flops 1024 | bytes 8192 | tf_op jit(solution)/shard_map/psum | solution.py:20
  183.4 1.6 add_reduce_fusion
  184.9 13.6 %pmax.55 = f32[384]{0:T(512)S(1)} all-reduce(f32[384]{0:T(512)S(1)} %add_reduce_fusion), channel_id=1, replica_groups=mesh['doc'=4,'cen'=8] {'cen'}, use_global_device_ids=true, to_apply=%region_25.0 | all-reduce | flops 384 | bytes 3072 | tf_op jit(solution)/shard_map/pmax | solution.py:12
  198.5 1.8 exponential_reduce_fusion
  200.3 13.6 %psum.62 = f32[384]{0:T(512)S(1)} all-reduce(f32[384]{0:T(512)S(1)} %exponential_reduce_fusion), channel_id=1, replica_groups=mesh['doc'=4,'cen'=8] {'cen'}, use_global_device_ids=true, to_apply=%region_27.0 | all-reduce | flops 384 | bytes 3072 | tf_op jit(solution)/shard_map/psum | solution.py:13
  213.9 1.8 fusion
  215.8 0.0 copy-start.1
  215.8 0.9 copy-done.1
  216.7 2.6 %convolution_convert_fusion = bf16[1024,1024]{1,0:T(8,128)(2,1)} fusion(bf16[384,1024]{1,0:T(8,128)(2,1)S(1)} %get-tuple-element.4, bf16[384,1024]{1,0:T(8,128)(2,1)S(1)} %all_gather.3), kind=kOutput, calls=%fused_computation | convolution fusion | flops 806354944 | bytes 3670016 | tf_op jit(solution)/shard_map/dot_general | solution.py:48
  219.3 0.0 reduce-scatter.2.cloned.1.call-update
  219.3 9.0 %psum.63 = f32[1024]{0:T(1024)S(1)} all-reduce(f32[1024]{0:T(1024)S(1)} %get-tuple-element.3), channel_id=1, replica_groups=mesh['doc'=4,'cen'=8] {'doc'}, use_global_device_ids=true, to_apply=%region_29.0 | all-reduce | flops 1024 | bytes 8192 | tf_op jit(solution)/shard_map/psum | solution.py:47
  228.4 0.6 broadcast_multiply_fusion
  229.0 22.9 %reduce-scatter.2.cloned.1.call-done = bf16[1024,256]{1,0:T(8,128)(2,1)} async-done(((bf16[1024,1024]{1,0:T(8,128)(2,1)}), bf16[1024,256]{1,0:T(8,128)(2,1)}) %reduce-scatter.2.cloned.1.call-update) | async-done | bytes 524304 | tf_op jit(solution)/shard_map/reduce_scatter | solution.py:51
  251.9 2.2 multiply_divide_fusion
  (7 shorter events, 0.1 us)
Async XLA Ops:
  7.2 17.6 %copy-start = (bf16[1024,1024]{1,0:T(8,128)(2,1)S(1)}, bf16[1024,1024]{1,0:T(8,128)(2,1)}, u32[]{:S(2)}) copy-start(bf16[1024,1024]{1,0:T(8,128)(2,1)} %param.3) | copy-start | bytes 6291460
  7.2 244.7 %reduce-scatter.2.cloned.1.call-start = ((), (), s32[]{:S(2)}) async-start(), calls=%async_computation.1 | async-start | bytes 2621440 | tf_op jit(solution)/shard_map/reduce_scatter | solution.py:51
  215.8 0.9 copy-start.1
Sparse Core Ops, SparseCore 0:
  219.4 32.4 reduce-scatter.1
where the time goes:
time: 262 us; the launch traced here: 261 us
  blocking collectives  191 us (73%)
  other arithmetic  26.7 us (10%)
  waiting for transfers between devices  23 us (9%)
  between operations  14.1 us (5%)
  matrix products  4.81 us (2%)
    pmax x4, blocking collectives, row_log_total(): peak = lax.pmax(local_max, 'cen')  57.8 us
    psum x4, blocking collectives, row_log_total(): total = lax.psum(jnp.sum(jnp.exp(shifted - peak[:, None]), axis=1), 'cen')  54.4 us
    pmax x3, blocking collectives, col_log_total(): peak = lax.pmax(local_max, 'doc')  28.6 us
    psum x3, blocking collectives, col_log_total(): total = lax.psum(jnp.sum(jnp.exp(shifted - peak[None, :]), axis=0), 'doc')  24.1 us
    reduce_scatter x1, waiting for transfers between devices, shards(): lax.psum_scatter(partial_value.astype(jnp.bfloat16), 'doc', scatter_dimen...  22.9 us
    all_gather x1, blocking collectives, shards(): group_rows = lax.all_gather(passages, 'cen', axis=0, tiled=True)  17.6 us
    psum x1, blocking collectives, shards(): raw_mass = lax.psum(jnp.sum(weights, axis=0), 'doc')  9.04 us
    reduce_sum x4, other arithmetic, row_log_total(): total = lax.psum(jnp.sum(jnp.exp(shifted - peak[:, None]), axis=1), 'cen')  7.19 us
  transfers between devices with their start and end apart: 1, of which 1 were waited for; matrix products, arithmetic and copies ran while one was open for 0% of the time, Pallas kernels for 0%

commit v1 on v0

--- a/solution.py
+++ b/solution.py
@@ -26,7 +26,15 @@
     doc_count = lax.axis_size("doc")
     width = passages.shape[1]
     scale = 1.0 / math.sqrt(width)
-    group_rows = lax.all_gather(passages, "cen", axis=0, tiled=True)
+    ways, here = (lax.axis_size("cen"), lax.axis_index("cen"))
+    grown, reach = (passages, 1)
+    while reach < ways:
+        theirs = lax.ppermute(grown, "cen", [(d, d ^ reach) for d in range(ways)])
+        mine_first = jnp.concatenate([grown, theirs], axis=0)
+        theirs_first = jnp.concatenate([theirs, grown], axis=0)
+        grown = jnp.where(here & reach == 0, mine_first, theirs_first)
+        reach = 2 * reach
+    group_rows = grown
     scores = (
         lax.dot_general(
             group_rows, centroids, (((1,), (1,)), ((), ())), preferred_element_type=jnp.float32

time: 262 us -> 274 us (1.046)
  waiting for transfers between devices: 23 us -> 46.6 us
  blocking collectives: 191 us -> 173 us
  starting transfers between devices: 0.04 us -> 6.37 us
    ppermute x0 -> x3, waiting for transfers between devices: none -> 23.6 us  [shards(): theirs = lax.ppermute(grown, 'cen', [(d, d ^ reach) for d in range(ways)])]
    all_gather x1 -> x0, blocking collectives: 17.6 us -> none  [shards(): group_rows = lax.all_gather(passages, 'cen', axis=0, tiled=True)]
    ppermute x0 -> x3, starting transfers between devices: none -> 6.33 us  [shards(): theirs = lax.ppermute(grown, 'cen', [(d, d ^ reach) for d in range(ways)])]
  transfers between devices with their start and end apart: 1 -> 4, of which waited for: 1 -> 4; matrix products, arithmetic and copies ran while one was open for 0% -> 0% of each run, Pallas kernels for 0% -> 0%
where the time goes in v1:
time: 274 us; the launch traced here: 273 us
  blocking collectives  173 us (63%)
  waiting for transfers between devices  46.6 us (17%)
  other arithmetic  27.8 us (10%)
  between operations  14.1 us (5%)
  starting transfers between devices  6.37 us (2%)
  matrix products  4.87 us (2%)
    pmax x4, blocking collectives, row_log_total(): peak = lax.pmax(local_max, 'cen')  57.3 us
    psum x4, blocking collectives, row_log_total(): total = lax.psum(jnp.sum(jnp.exp(shifted - peak[:, None]), axis=1), 'cen')  54.4 us
    pmax x3, blocking collectives, col_log_total(): peak = lax.pmax(local_max, 'doc')  28.6 us
    psum x3, blocking collectives, col_log_total(): total = lax.psum(jnp.sum(jnp.exp(shifted - peak[None, :]), axis=0), 'doc')  24.1 us
    ppermute x3, waiting for transfers between devices, shards(): theirs = lax.ppermute(grown, 'cen', [(d, d ^ reach) for d in range(ways)])  23.6 us
    reduce_scatter x1, waiting for transfers between devices, shards(): lax.psum_scatter(partial_value.astype(jnp.bfloat16), 'doc', scatter_dimen...  22.9 us
    psum x1, blocking collectives, shards(): raw_mass = lax.psum(jnp.sum(weights, axis=0), 'doc')  9.04 us
    reduce_sum x4, other arithmetic, row_log_total(): total = lax.psum(jnp.sum(jnp.exp(shifted - peak[:, None]), axis=1), 'cen')  7.19 us
  transfers between devices with their start and end apart: 4, of which 4 were waited for; matrix products, arithmetic and copies ran while one was open for 0% of the time, Pallas kernels for 0%

profile of v1, /device:TPU:0, one launch (start us, length us, event | category | flops | bytes accessed | tf_op | source)
XLA Modules:
  0.0 273.2 jit_solution(15502789089456203110)
XLA Ops:
  7.2 0.0 copy-start
  7.2 0.0 reduce-scatter.2.cloned.1.call-start
  7.2 0.5 collective-permute-start
  7.7 1.2 collective-permute-done
  8.9 1.0 maximum_select_fusion.2
  9.9 3.0 %collective-permute-start.1 = (bf16[96,1024]{1,0:T(8,128)(2,1)S(1)}, bf16[96,1024]{1,0:T(8,128)(2,1)S(1)}, u32[]{:S(2)}, u32[]{:S(2)}) collective-permute-start(bf16[96,1024]{1,0:T(8,128)(2,1)S(1)} %maximum_select_fusion.2), channel_id=1, source_target_pairs={{0,2},{1,3},{2,0},{3,1},{4,6},{5,7},{6,4},{7,5},{8,10},{9,11},{10,... | collective-permute-start | bytes 589832 | tf_op jit(solution)/shard_map/ppermute | solution.py:32
  12.9 5.2 %collective-permute-done.1 = bf16[96,1024]{1,0:T(8,128)(2,1)S(1)} collective-permute-done((bf16[96,1024]{1,0:T(8,128)(2,1)S(1)}, bf16[96,1024]{1,0:T(8,128)(2,1)S(1)}, u32[]{:S(2)}, u32[]{:S(2)}) %collective-permute-start.1) | collective-permute-done | bytes 196640 | tf_op jit(solution)/shard_map/ppermute | solution.py:32
  18.1 0.1 maximum_select_fusion.1
  18.2 2.8 %collective-permute-start.2 = (bf16[192,1024]{1,0:T(8,128)(2,1)S(1)}, bf16[192,1024]{1,0:T(8,128)(2,1)S(1)}, u32[]{:S(2)}, u32[]{:S(2)}) collective-permute-start(bf16[192,1024]{1,0:T(8,128)(2,1)S(1)} %maximum_select_fusion.1), channel_id=1, source_target_pairs={{0,4},{1,5},{2,6},{3,7},{4,0},{5,1},{6,2},{7,3},{8,12},{9,13},{10,... | collective-permute-start | bytes 1179656 | tf_op jit(solution)/shard_map/ppermute | solution.py:32
  21.0 17.2 %collective-permute-done.2 = bf16[192,1024]{1,0:T(8,128)(2,1)S(1)} collective-permute-done((bf16[192,1024]{1,0:T(8,128)(2,1)S(1)}, bf16[192,1024]{1,0:T(8,128)(2,1)S(1)}, u32[]{:S(2)}, u32[]{:S(2)}) %collective-permute-start.2) | collective-permute-done | bytes 393248 | tf_op jit(solution)/shard_map/ppermute | solution.py:32
  38.3 0.0 copy-done
  38.3 0.0 copy-start.2
  38.3 2.2 fusion.3
  40.5 0.0 copy-done.2
  40.5 16.5 %pmax.49 = f32[384]{0:T(512)S(1)} all-reduce(f32[384]{0:T(512)S(1)} %get-tuple-element.5), channel_id=1, replica_groups=mesh['doc'=4,'cen'=8] {'cen'}, use_global_device_ids=true, to_apply=%region_1.2 | all-reduce | flops 384 | bytes 3072 | tf_op jit(solution)/shard_map/pmax | solution.py:12
  57.0 1.8 exponential_reduce_fusion.6
  58.8 13.6 %psum.56 = f32[384]{0:T(512)S(1)} all-reduce(f32[384]{0:T(512)S(1)} %exponential_reduce_fusion.6), channel_id=1, replica_groups=mesh['doc'=4,'cen'=8] {'cen'}, use_global_device_ids=true, to_apply=%region_3.4 | all-reduce | flops 384 | bytes 3072 | tf_op jit(solution)/shard_map/psum | solution.py:13
  72.4 1.6 add_reduce_fusion.5
  74.0 9.9 %pmax.50 = f32[1024]{0:T(1024)S(1)} all-reduce(f32[1024]{0:T(1024)S(1)} %add_reduce_fusion.5), channel_id=1, replica_groups=mesh['doc'=4,'cen'=8] {'doc'}, use_global_device_ids=true, to_apply=%region_5.6 | all-reduce | flops 1024 | bytes 8192 | tf_op jit(solution)/shard_map/pmax | solution.py:19
  83.9 1.7 exponential_reduce_fusion.5
  85.6 8.0 %psum.57 = f32[1024]{0:T(1024)S(1)} all-reduce(f32[1024]{0:T(1024)S(1)} %exponential_reduce_fusion.5), channel_id=1, replica_groups=mesh['doc'=4,'cen'=8] {'doc'}, use_global_device_ids=true, to_apply=%region_7.8 | all-reduce | flops 1024 | bytes 8192 | tf_op jit(solution)/shard_map/psum | solution.py:20
  93.7 1.6 add_reduce_fusion.4
  95.3 13.6 %pmax.51 = f32[384]{0:T(512)S(1)} all-reduce(f32[384]{0:T(512)S(1)} %add_reduce_fusion.4), channel_id=1, replica_groups=mesh['doc'=4,'cen'=8] {'cen'}, use_global_device_ids=true, to_apply=%region_9.10 | all-reduce | flops 384 | bytes 3072 | tf_op jit(solution)/shard_map/pmax | solution.py:12
  108.8 1.8 exponential_reduce_fusion.4
  110.6 13.6 %psum.58 = f32[384]{0:T(512)S(1)} all-reduce(f32[384]{0:T(512)S(1)} %exponential_reduce_fusion.4), channel_id=1, replica_groups=mesh['doc'=4,'cen'=8] {'cen'}, use_global_device_ids=true, to_apply=%region_11.12 | all-reduce | flops 384 | bytes 3072 | tf_op jit(solution)/shard_map/psum | solution.py:13
  124.2 1.6 add_reduce_fusion.3
  125.8 9.0 %pmax.52 = f32[1024]{0:T(1024)S(1)} all-reduce(f32[1024]{0:T(1024)S(1)} %add_reduce_fusion.3), channel_id=1, replica_groups=mesh['doc'=4,'cen'=8] {'doc'}, use_global_device_ids=true, to_apply=%region_13.14 | all-reduce | flops 1024 | bytes 8192 | tf_op jit(solution)/shard_map/pmax | solution.py:19
  134.8 1.7 exponential_reduce_fusion.3
  136.5 8.1 %psum.59 = f32[1024]{0:T(1024)S(1)} all-reduce(f32[1024]{0:T(1024)S(1)} %exponential_reduce_fusion.3), channel_id=1, replica_groups=mesh['doc'=4,'cen'=8] {'doc'}, use_global_device_ids=true, to_apply=%region_15.16 | all-reduce | flops 1024 | bytes 8192 | tf_op jit(solution)/shard_map/psum | solution.py:20
  144.6 1.6 add_reduce_fusion.2
  146.2 13.6 %pmax.53 = f32[384]{0:T(512)S(1)} all-reduce(f32[384]{0:T(512)S(1)} %add_reduce_fusion.2), channel_id=1, replica_groups=mesh['doc'=4,'cen'=8] {'cen'}, use_global_device_ids=true, to_apply=%region_17.18 | all-reduce | flops 384 | bytes 3072 | tf_op jit(solution)/shard_map/pmax | solution.py:12
  159.8 1.8 exponential_reduce_fusion.2
  161.6 13.6 %psum.60 = f32[384]{0:T(512)S(1)} all-reduce(f32[384]{0:T(512)S(1)} %exponential_reduce_fusion.2), channel_id=1, replica_groups=mesh['doc'=4,'cen'=8] {'cen'}, use_global_device_ids=true, to_apply=%region_19.20 | all-reduce | flops 384 | bytes 3072 | tf_op jit(solution)/shard_map/psum | solution.py:13
  175.2 1.6 add_reduce_fusion.1
  176.8 9.7 %pmax.54 = f32[1024]{0:T(1024)S(1)} all-reduce(f32[1024]{0:T(1024)S(1)} %add_reduce_fusion.1), channel_id=1, replica_groups=mesh['doc'=4,'cen'=8] {'doc'}, use_global_device_ids=true, to_apply=%region_21.22 | all-reduce | flops 1024 | bytes 8192 | tf_op jit(solution)/shard_map/pmax | solution.py:19
  186.5 1.7 exponential_reduce_fusion.1
  188.3 8.1 %psum.61 = f32[1024]{0:T(1024)S(1)} all-reduce(f32[1024]{0:T(1024)S(1)} %exponential_reduce_fusion.1), channel_id=1, replica_groups=mesh['doc'=4,'cen'=8] {'doc'}, use_global_device_ids=true, to_apply=%region_23.24 | all-reduce | flops 1024 | bytes 8192 | tf_op jit(solution)/shard_map/psum | solution.py:20
  196.3 1.6 add_reduce_fusion
  197.9 13.6 %pmax.55 = f32[384]{0:T(512)S(1)} all-reduce(f32[384]{0:T(512)S(1)} %add_reduce_fusion), channel_id=1, replica_groups=mesh['doc'=4,'cen'=8] {'cen'}, use_global_device_ids=true, to_apply=%region_25.26 | all-reduce | flops 384 | bytes 3072 | tf_op jit(solution)/shard_map/pmax | solution.py:12
  211.5 1.8 exponential_reduce_fusion
  213.3 13.6 %psum.62 = f32[384]{0:T(512)S(1)} all-reduce(f32[384]{0:T(512)S(1)} %exponential_reduce_fusion), channel_id=1, replica_groups=mesh['doc'=4,'cen'=8] {'cen'}, use_global_device_ids=true, to_apply=%region_27.28 | all-reduce | flops 384 | bytes 3072 | tf_op jit(solution)/shard_map/psum | solution.py:13
  226.9 0.0 copy-start.3
  226.9 1.9 fusion
  228.8 0.0 copy-start.1
  228.8 0.0 copy-done.3
  228.8 2.7 convolution_convert_fusion
  231.5 0.0 copy-done.1
  231.5 0.0 reduce-scatter.2.cloned.1.call-update
  231.5 9.0 %psum.63 = f32[1024]{0:T(1024)S(1)} all-reduce(f32[1024]{0:T(1024)S(1)} %get-tuple-element.3), channel_id=1, replica_groups=mesh['doc'=4,'cen'=8] {'doc'}, use_global_device_ids=true, to_apply=%region_29.30 | all-reduce | flops 1024 | bytes 8192 | tf_op jit(solution)/shard_map/psum | solution.py:55
  240.6 0.6 broadcast_multiply_fusion
  241.2 22.9 %reduce-scatter.2.cloned.1.call-done = bf16[1024,256]{1,0:T(8,128)(2,1)} async-done(((bf16[1024,1024]{1,0:T(8,128)(2,1)}), bf16[1024,256]{1,0:T(8,128)(2,1)}) %reduce-scatter.2.cloned.1.call-update) | async-done | bytes 524304 | tf_op jit(solution)/shard_map/reduce_scatter | solution.py:59
  264.1 2.2 multiply_divide_fusion
  (7 shorter events, 0.1 us)
Async XLA Ops:
  7.2 31.1 %copy-start = (bf16[1024,1024]{1,0:T(8,128)(2,1)S(1)}, bf16[1024,1024]{1,0:T(8,128)(2,1)}, u32[]{:S(2)}) copy-start(bf16[1024,1024]{1,0:T(8,128)(2,1)} %param.3) | copy-start | bytes 6291460
  7.2 256.9 %reduce-scatter.2.cloned.1.call-start = ((), (), s32[]{:S(2)}) async-start(), calls=%async_computation.1 | async-start | bytes 2621440 | tf_op jit(solution)/shard_map/reduce_scatter | solution.py:59
  7.2 1.7 collective-permute-start
  9.9 8.2 %collective-permute-start.1 = (bf16[96,1024]{1,0:T(8,128)(2,1)S(1)}, bf16[96,1024]{1,0:T(8,128)(2,1)S(1)}, u32[]{:S(2)}, u32[]{:S(2)}) collective-permute-start(bf16[96,1024]{1,0:T(8,128)(2,1)S(1)} %maximum_select_fusion.2), channel_id=1, source_target_pairs={{0,2},{1,3},{2,0},{3,1},{4,6},{5,7},{6,4},{7,5},{8,10},{9,11},{10,... | collective-permute-start | bytes 589832 | tf_op jit(solution)/shard_map/ppermute | solution.py:32
  18.2 20.1 %collective-permute-start.2 = (bf16[192,1024]{1,0:T(8,128)(2,1)S(1)}, bf16[192,1024]{1,0:T(8,128)(2,1)S(1)}, u32[]{:S(2)}, u32[]{:S(2)}) collective-permute-start(bf16[192,1024]{1,0:T(8,128)(2,1)S(1)} %maximum_select_fusion.1), channel_id=1, source_target_pairs={{0,4},{1,5},{2,6},{3,7},{4,0},{5,1},{6,2},{7,3},{8,12},{9,13},{10,... | collective-permute-start | bytes 1179656 | tf_op jit(solution)/shard_map/ppermute | solution.py:32
  38.3 2.2 copy-start.2
  226.9 1.9 copy-start.3
  228.8 2.7 copy-start.1
Sparse Core Ops, SparseCore 0:
  231.6 32.4 reduce-scatter.1
